TPU v7x, 128 devices: a whole 4x4x4 slice. The times are simulated.
128 devices in a mesh: row: 16 (over y, x), col: 4 (over z), dp: 2 (over core).
Axes of the slice: x: 4, y: 4, z: 4, core: 2. Of those that a mesh axis runs over, the one named last changes fastest.
Arguments:
- inputs: bfloat16 [1024, 8192], P(('col', 'dp'), 'row'), may hold values from -6 to 6
- gate_weight: bfloat16 [8192, 14336], P('row', 'col'), may hold values from -0.0625 to 0.0625
- up_weight: bfloat16 [8192, 14336], P('row', 'col'), may hold values from -0.0625 to 0.0625
- down_weight: bfloat16 [14336, 8192], P('col', 'row'), may hold values from -0.046875 to 0.046875
- reward_head: bfloat16 [8192], P('row'), may hold values from -0.0625 to 0.0625
- upstream: bfloat16 [1024, 8192], P(('col', 'dp'), 'row'), may hold values from -0.59765625 to 0.59765625
- labels: int32 [1024], P(('col', 'dp')), may hold values from 0 to 1
- label_mask: int32 [1024], P(('col', 'dp')), may hold values 0 or 1
Outputs:
- gate_grad: float32 [8192, 14336], P(('row', 'dp'), 'col')
- up_grad: float32 [8192, 14336], P(('row', 'dp'), 'col')
- down_grad: float32 [14336, 8192], P(('col', 'dp'), 'row')
- input_grad: float32 [1024, 8192], P(('col', 'dp'), 'row')
All inputs are finite; a program needn't handle non-finite values. No bound on the sum of `label_mask` on one device may be relied on, other than what follows from the above.
Results may differ from a plain program's by a relative error of at most 0.035.
Values may be sent and summed in bfloat16 or wider, within the bound.
No kernel may reach another device: no remote copies, remote signals or barrier semaphores. Data moves between devices by JAX's collectives and lax.ppermute only.
A program may use at most 128 MiB of HBM per device.

v0:
```python
import jax
import jax.numpy as jnp
from jax import lax
from jax.sharding import PartitionSpec as P

reward_weight = 8.0


def transpose_product(left, right):
    return lax.dot_general(
        left, right, (((0,), (0,)), ((), ())), preferred_element_type=jnp.float32
    )


def right_transpose(left, right):
    return lax.dot_general(
        left, right, (((1,), (1,)), ((), ())), preferred_element_type=jnp.float32
    )


def gather_tokens(block):
    return lax.all_gather(block, "col", axis=0, tiled=True)


def gather_hidden(stacked):
    return lax.all_gather(stacked, "row", axis=1, tiled=True)


def column_total(term_fn, count_rows):
    return lax.psum_scatter(
        term_fn(jnp.int32(0), count_rows * lax.axis_size("col")).astype(jnp.bfloat16),
        "col",
        scatter_dimension=0,
        tiled=True,
    ).astype(jnp.float32)


def per_device(
    inputs, gate_weight, up_weight, down_weight, reward_head, upstream, labels, label_mask
):
    width = gate_weight.shape[1]
    gathered = gather_tokens(inputs)
    rows = gathered
    joined = lax.psum_scatter(
        jnp.concatenate(
            [
                jnp.dot(rows, gate_weight, preferred_element_type=jnp.float32),
                jnp.dot(rows, up_weight, preferred_element_type=jnp.float32),
            ],
            axis=1,
        ).astype(jnp.bfloat16),
        "row",
        scatter_dimension=0,
        tiled=True,
    ).astype(jnp.float32)
    gate = joined[:, :width]
    upper = joined[:, width:]
    sigmoid_gate = jax.nn.sigmoid(gate)
    hidden = (gate * sigmoid_gate * upper).astype(jnp.bfloat16)
    hidden_all = gather_hidden(hidden[None])[0]

    def output_term(start, count):
        return jnp.dot(hidden_all, down_weight, preferred_element_type=jnp.float32)

    mixed = column_total(output_term, inputs.shape[0])
    outcome = inputs.astype(jnp.float32) + mixed
    head_value = reward_head.astype(jnp.float32)
    partial_score = jnp.dot(outcome, head_value, precision=lax.Precision.HIGHEST)
    score = lax.psum(partial_score, "row")
    slope = (
        reward_weight
        * label_mask.astype(jnp.float32)
        * (jax.nn.sigmoid(score) - labels.astype(jnp.float32))
    )
    grad_out = upstream.astype(jnp.float32) + slope[:, None] * head_value[None, :]
    grad_mixed = grad_out.astype(jnp.bfloat16)
    grad_rows = gather_tokens(grad_mixed)
    rows = grad_rows
    grad_hidden = lax.psum_scatter(
        right_transpose(rows, down_weight).astype(jnp.bfloat16),
        "row",
        scatter_dimension=0,
        tiled=True,
    ).astype(jnp.float32)
    grad_gate = (grad_hidden * upper * sigmoid_gate * (1.0 + gate * (1.0 - sigmoid_gate))).astype(
        jnp.bfloat16
    )
    grad_upper = (grad_hidden * gate * sigmoid_gate).astype(jnp.bfloat16)
    grads_all = gather_hidden(jnp.stack([grad_gate, grad_upper]))

    def input_term(start, count):
        return right_transpose(grads_all[0], gate_weight) + right_transpose(grads_all[1], up_weight)

    input_grad = grad_out + column_total(input_term, inputs.shape[0])
    gate_grad, up_grad, down_grad = (
        lax.psum_scatter(
            transpose_product(gathered, grads_all[0]).astype(jnp.bfloat16),
            "dp",
            scatter_dimension=0,
            tiled=True,
        ).astype(jnp.float32),
        lax.psum_scatter(
            transpose_product(gathered, grads_all[1]).astype(jnp.bfloat16),
            "dp",
            scatter_dimension=0,
            tiled=True,
        ).astype(jnp.float32),
        lax.psum_scatter(
            transpose_product(hidden_all, grad_rows).astype(jnp.bfloat16),
            "dp",
            scatter_dimension=0,
            tiled=True,
        ).astype(jnp.float32),
    )
    return (gate_grad, up_grad, down_grad, input_grad)


def solution(mesh):
    in_specs = (
        P(("col", "dp"), "row"),
        P("row", "col"),
        P("row", "col"),
        P("col", "row"),
        P("row"),
        P(("col", "dp"), "row"),
        P(("col", "dp")),
        P(("col", "dp")),
    )
    out_specs = (
        P(("row", "dp"), "col"),
        P(("row", "dp"), "col"),
        P(("col", "dp"), "row"),
        P(("col", "dp"), "row"),
    )
    return jax.shard_map(
        per_device, mesh=mesh, in_specs=in_specs, out_specs=out_specs, check_vma=False
    )
```

profile of v0, /device:TPU:1, one launch (start us, length us, event | category | flops | bytes accessed | tf_op | source)
XLA Modules:
  0.0 488.5 jit_solution(17730826505208931112)
XLA Ops:
  7.2 13.6 %all_gather.12 = bf16[512,512]{1,0:T(8,128)(2,1)S(1)} all-gather(bf16[128,512]{1,0:T(8,128)(2,1)} %param.8), channel_id=1, replica_groups=mesh['row'=16,'col'=4,'dp'=2] {'col'}, dimensions={0}, use_global_device_ids=true | all-gather | bytes 655360 | tf_op jit(solution)/shard_map/all_gather | solution.py:22
  20.8 4.3 convolution_convert_fusion.4
  25.1 3.9 convolution_convert_fusion.5
  29.0 6.0 %pad_maximum_fusion = bf16[512,7168]{1,0:T(8,128)(2,1)} fusion(bf16[512,3584]{1,0:T(8,128)(2,1)S(1)} %convolution_convert_fusion.4, bf16[512,3584]{1,0:T(8,128)(2,1)} %convolution_convert_fusion.5), kind=kLoop, calls=%fused_computation | loop fusion | flops 14680064 | bytes 14680064 | tf_op jit(solution)/shard_map/concatenate | solution.py:45
  35.1 84.9 %reduce-scatter.8.cloned.1.call-done = bf16[32,7168]{1,0:T(8,128)(2,1)} async-done(((bf16[512,7168]{1,0:T(8,128)(2,1)}), bf16[32,7168]{1,0:T(8,128)(2,1)}) %reduce-scatter.8.cloned.1.call-update) | async-done | bytes 458768 | tf_op jit(solution)/shard_map/reduce_scatter | solution.py:44
  122.0 50.6 %all-gather.6.cloned.1.call-done = bf16[512,3584]{1,0:T(8,128)(2,1)} async-done(((bf16[32,3584]{1,0:T(8,128)(2,1)}), bf16[512,3584]{1,0:T(8,128)(2,1)}) %all-gather.6.cloned.1.call-update) | async-done | bytes 3670032 | tf_op jit(solution)/shard_map/all_gather | solution.py:26
  172.7 6.0 %convolution_convert_fusion.6 = bf16[512,512]{1,0:T(8,128)(2,1)} fusion(bf16[512,3584]{1,0:T(8,128)(2,1)} %all-gather.6.cloned.1.call-done, bf16[3584,512]{1,0:T(8,128)(2,1)} %param.11), kind=kOutput, calls=%fused_computation.15 | convolution fusion | flops 1879310336 | bytes 7864320 | tf_op jit(solution)/shard_map/dot_general | solution.py:63
  178.8 19.6 %reduce-scatter.10.cloned.1.call-done = bf16[128,512]{1,0:T(8,128)(2,1)} async-done(((bf16[512,512]{1,0:T(8,128)(2,1)}), bf16[128,512]{1,0:T(8,128)(2,1)}) %reduce-scatter.10.cloned.1.call-update) | async-done | bytes 131088 | tf_op jit(solution)/shard_map/reduce_scatter | solution.py:30
  199.5 33.2 %psum.7 = f32[128]{0:T(128)S(1)} all-reduce(f32[128]{0:T(128)S(1)} %convolution_bitcast_fusion), channel_id=1, replica_groups=mesh['row'=16,'col'=4,'dp'=2] {'row'}, use_global_device_ids=true, to_apply=%region_2.0 | all-reduce | flops 128 | bytes 1024 | tf_op jit(solution)/shard_map/psum | solution.py:69
  232.8 10.2 %all_gather.14 = bf16[512,512]{1,0:T(8,128)(2,1)S(1)} all-gather(bf16[128,512]{1,0:T(8,128)(2,1)S(1)} %fusion.14), channel_id=1, replica_groups=mesh['row'=16,'col'=4,'dp'=2] {'col'}, dimensions={0}, use_global_device_ids=true | all-gather | bytes 655360 | tf_op jit(solution)/shard_map/all_gather | solution.py:22
  243.0 6.0 %convolution_convert_fusion.3 = bf16[512,3584]{1,0:T(8,128)(2,1)} fusion(bf16[512,512]{1,0:T(8,128)(2,1)S(1)} %all_gather.14, bf16[3584,512]{1,0:T(8,128)(2,1)} %param.11), kind=kOutput, calls=%fused_computation.4 | convolution fusion | flops 1880883200 | bytes 7864320 | tf_op jit(solution)/shard_map/dot_general | solution.py:16
  249.1 81.0 %reduce-scatter.12.cloned.1.call-done = bf16[32,3584]{1,0:T(8,128)(2,1)} async-done(((bf16[512,3584]{1,0:T(8,128)(2,1)}), bf16[32,3584]{1,0:T(8,128)(2,1)}) %reduce-scatter.12.cloned.1.call-update) | async-done | bytes 229392 | tf_op jit(solution)/shard_map/reduce_scatter | solution.py:79
  332.1 6.0 %convolution_convert_fusion = bf16[3584,512]{1,0:T(8,128)(2,1)} fusion(bf16[512,3584]{1,0:T(8,128)(2,1)} %all-gather.6.cloned.1.call-done, bf16[512,512]{1,0:T(8,128)(2,1)S(1)} %all_gather.14), kind=kOutput, calls=%fused_computation.1 | convolution fusion | flops 1880883200 | bytes 7864320 | tf_op jit(solution)/shard_map/dot_general | solution.py:10
  338.1 61.8 %all-gather.4.cloned.1.call-done = bf16[2,512,3584]{2,1,0:T(8,128)(2,1)} async-done(((bf16[2,32,3584]{2,1,0:T(8,128)(2,1)}), bf16[2,512,3584]{2,1,0:T(8,128)(2,1)}) %all-gather.4.cloned.1.call-update) | async-done | bytes 7340048 | tf_op jit(solution)/shard_map/all_gather | solution.py:26
  399.9 5.4 %fusion.2 = f32[512,512]{1,0:T(8,128)S(1)} fusion(bf16[512,3584]{1,0:T(8,128)(2,1)} %param.9, bf16[2,512,3584]{2,1,0:T(8,128)(2,1)} %all-gather.4.cloned.1.call-done), kind=kOutput, calls=%fused_computation.11 | convolution fusion | flops 1879048192 | bytes 8388608 | tf_op jit(solution)/shard_map/dot_general | solution.py:16
  406.1 2.9 fusion.5
  409.3 6.0 %fusion.1 = bf16[512,3584]{0,1:T(8,128)(2,1)} fusion(bf16[512,512]{1,0:T(8,128)(2,1)S(1)} %all_gather.12, bf16[2,512,3584]{2,1,0:T(8,128)(2,1)} %all-gather.4.cloned.1.call-done), kind=kOutput, calls=%fused_computation.8 | convolution fusion | flops 1880883200 | bytes 7864320 | tf_op jit(solution)/shard_map/dot_general | solution.py:10
  415.4 6.3 %fusion = bf16[512,3584]{0,1:T(8,128)(2,1)} fusion(bf16[512,512]{1,0:T(8,128)(2,1)S(1)} %all_gather.12, bf16[2,512,3584]{2,1,0:T(8,128)(2,1)} %all-gather.4.cloned.1.call-done), kind=kOutput, calls=%fused_computation.7 | convolution fusion | flops 1880883200 | bytes 7864320 | tf_op jit(solution)/shard_map/dot_general | solution.py:10
  421.7 3.9 convert_element_type.94
  425.5 14.9 %reduce-scatter.20.cloned.1.call-done = bf16[128,512]{1,0:T(8,128)(2,1)} async-done(((bf16[512,512]{1,0:T(8,128)(2,1)}), bf16[128,512]{1,0:T(8,128)(2,1)}) %reduce-scatter.20.cloned.1.call-update) | async-done | bytes 131088 | tf_op jit(solution)/shard_map/reduce_scatter | solution.py:30
  442.2 17.1 %reduce-scatter.16.cloned.1.call-done = bf16[256,3584]{0,1:T(8,128)(2,1)} async-done(((bf16[512,3584]{0,1:T(8,128)(2,1)}), bf16[256,3584]{0,1:T(8,128)(2,1)}) %reduce-scatter.16.cloned.1.call-update) | async-done | bytes 1835024 | tf_op jit(solution)/shard_map/reduce_scatter | solution.py:102
  459.3 4.0 copy.13
  463.3 14.7 %reduce-scatter.14.cloned.1.call-done = bf16[256,3584]{0,1:T(8,128)(2,1)} async-done(((bf16[512,3584]{0,1:T(8,128)(2,1)}), bf16[256,3584]{0,1:T(8,128)(2,1)}) %reduce-scatter.14.cloned.1.call-update) | async-done | bytes 1835024 | tf_op jit(solution)/shard_map/reduce_scatter | solution.py:96
  478.0 4.0 copy.12
  (45 shorter events, 8.4 us)
Async XLA Ops:
  7.2 112.8 %reduce-scatter.8.cloned.1.call-start = ((), (), s32[]{:S(2)}) async-start(), calls=%async_computation.7 | async-start | bytes 7798784 | tf_op jit(solution)/shard_map/reduce_scatter | solution.py:44
  20.8 4.3 copy-start.6
  35.0 137.6 %all-gather.6.cloned.1.call-start = ((), (), s32[]{:S(2)}) async-start(), calls=%async_computation.15 | async-start | bytes 3899392 | tf_op jit(solution)/shard_map/all_gather | solution.py:26
  121.9 56.8 %copy-start.2 = (bf16[512]{0:T(512)(128)(2,1)S(1)}, bf16[512]{0:T(512)(128)(2,1)}, u32[]{:S(2)}) copy-start(bf16[512]{0:T(512)(128)(2,1)} %param.12) | copy-start | bytes 3076
  121.9 76.5 %copy-start = (bf16[128,512]{1,0:T(8,128)(2,1)S(1)}, bf16[128,512]{1,0:T(8,128)(2,1)}, u32[]{:S(2)}) copy-start(bf16[128,512]{1,0:T(8,128)(2,1)} %param.8) | copy-start | bytes 393220
  122.0 110.7 %copy-start.3 = (s32[128]{0:T(128)S(1)}, s32[128]{0:T(128)}, u32[]{:S(2)}) copy-start(s32[128]{0:T(128)} %param.14) | copy-start | bytes 1540
  122.0 110.7 %copy-start.4 = (s32[128]{0:T(128)S(1)}, s32[128]{0:T(128)}, u32[]{:S(2)}) copy-start(s32[128]{0:T(128)} %param.15) | copy-start | bytes 1540
  122.0 110.7 %copy-start.1 = (bf16[128,512]{1,0:T(8,128)(2,1)S(1)}, bf16[128,512]{1,0:T(8,128)(2,1)}, u32[]{:S(2)}) copy-start(bf16[128,512]{1,0:T(8,128)(2,1)} %param.13) | copy-start | bytes 393220
  122.0 76.4 %reduce-scatter.10.cloned.1.call-start = ((), (), s32[]{:S(2)}) async-start(), calls=%async_computation.8 | async-start | bytes 655360 | tf_op jit(solution)/shard_map/reduce_scatter | solution.py:30
  178.7 151.3 %reduce-scatter.12.cloned.1.call-start = ((), (), s32[]{:S(2)}) async-start(), calls=%async_computation.9 | async-start | bytes 3899392 | tf_op jit(solution)/shard_map/reduce_scatter | solution.py:79
  249.0 150.9 %all-gather.4.cloned.1.call-start = ((), (), s32[]{:S(2)}) async-start(), calls=%async_computation.10 | async-start | bytes 7798784 | tf_op jit(solution)/shard_map/all_gather | solution.py:26
  332.0 89.7 %reduce-scatter.18.cloned.1.call-start = ((), (), s32[]{:S(2)}) async-start(), calls=%async_computation.13 | async-start | bytes 5505024 | tf_op jit(solution)/shard_map/reduce_scatter | solution.py:108
  338.1 102.4 %reduce-scatter.20.cloned.1.call-start = ((), (), s32[]{:S(2)}) async-start(), calls=%async_computation.14 | async-start | bytes 655360 | tf_op jit(solution)/shard_map/reduce_scatter | solution.py:30
  399.9 5.4 %copy-start.5 = (bf16[2,512,3584]{2,1,0:T(8,128)(2,1)S(1)}, bf16[2,512,3584]{2,1,0:T(8,128)(2,1)}, u32[]{:S(2)}) copy-start(bf16[2,512,3584]{2,1,0:T(8,128)(2,1)} %all-gather.4.cloned.1.call-done) | copy-start | bytes 22020100
  399.9 6.3 %copy-start.7 = (bf16[512,3584]{1,0:T(8,128)(2,1)S(1)}, bf16[512,3584]{1,0:T(8,128)(2,1)}, u32[]{:S(2)}) copy-start(bf16[512,3584]{1,0:T(8,128)(2,1)} %param.10) | copy-start | bytes 11010052
  409.1 50.3 %reduce-scatter.16.cloned.1.call-start = ((), (), s32[]{:S(2)}) async-start(), calls=%async_computation.12 | async-start | bytes 5505024 | tf_op jit(solution)/shard_map/reduce_scatter | solution.py:102
  415.3 62.7 %reduce-scatter.14.cloned.1.call-start = ((), (), s32[]{:S(2)}) async-start(), calls=%async_computation.11 | async-start | bytes 5505024 | tf_op jit(solution)/shard_map/reduce_scatter | solution.py:96
Sparse Core Ops, SparseCore 0:
  35.1 84.8 reduce-scatter.7
  122.9 49.6 all-gather.5
  178.8 19.5 reduce-scatter.9
  249.1 80.8 reduce-scatter.11
  332.8 67.0 all-gather.3
  402.8 14.3 reduce-scatter.17
  419.6 20.8 reduce-scatter.19
  443.4 15.8 reduce-scatter.15
  462.4 15.5 reduce-scatter.13
where the time goes:
time: 489 us; the launch traced here: 488 us
  waiting for transfers between devices  345 us (71%)
  blocking collectives  56.9 us (12%)
  matrix products  47.8 us (10%)
  other arithmetic  15.5 us (3%)
  between operations  14 us (3%)
  local copies, waits for them, and re-layouts  8.87 us (2%)
    all_gather x2, waiting for transfers between devices, gather_hidden(): return lax.all_gather(stacked, 'row', axis=1, tiled=True)  112 us
    reduce_scatter x1, waiting for transfers between devices, per_device(): lax.psum_scatter(jnp.concatenate([jnp.dot(rows, gate_weight, preferred_el...  84.9 us
    reduce_scatter x1, waiting for transfers between devices, per_device(): lax.psum_scatter(right_transpose(rows, down_weight).astype(jnp.bfloat16),...  81 us
    reduce_scatter x2, waiting for transfers between devices, column_total(): lax.psum_scatter(term_fn(jnp.int32(0), count_rows * lax.axis_size('col'))...  34.6 us
    psum x1, blocking collectives, per_device(): score = lax.psum(partial_score, 'row')  33.2 us
    all_gather x2, blocking collectives, gather_tokens(): return lax.all_gather(block, 'col', axis=0, tiled=True)  23.8 us
    dot_general x3, matrix products, transpose_product(): lax.dot_general(left, right, (((0,), (0,)), ((), ())), preferred_element_...  18.2 us
    reduce_scatter x1, waiting for transfers between devices, per_device(): lax.psum_scatter(transpose_product(gathered, grads_all[1]).astype(jnp.bfl...  17.1 us
  transfers between devices with their start and end apart: 9, of which 8 were waited for; matrix products, arithmetic and copies ran while one was open for 7% of the time, Pallas kernels for 0%

commit v1 on v0

--- a/solution.py
+++ b/solution.py
@@ -66,7 +66,7 @@
     outcome = inputs.astype(jnp.float32) + mixed
     head_value = reward_head.astype(jnp.float32)
     partial_score = jnp.dot(outcome, head_value, precision=lax.Precision.HIGHEST)
-    score = lax.psum(partial_score, "row")
+    score = jnp.sum(lax.all_gather(partial_score, "row"), axis=0)
     slope = (
         reward_weight
         * label_mask.astype(jnp.float32)

time: 489 us -> 473 us (0.967)
  blocking collectives: 56.9 us -> 39.8 us
    psum x1 -> x0, blocking collectives: 33.2 us -> none  [per_device(): score = lax.psum(partial_score, 'row')]
    all_gather x0 -> x1, blocking collectives: none -> 16.3 us  [per_device(): score = jnp.sum(lax.all_gather(partial_score, 'row'), axis=0)]
  transfers between devices with their start and end apart: 9 -> 9, of which waited for: 8 -> 8; matrix products, arithmetic and copies ran while one was open for 7% -> 8% of each run, Pallas kernels for 0% -> 0%
where the time goes in v1:
time: 473 us; the launch traced here: 472 us
  waiting for transfers between devices  345 us (73%)
  matrix products  47.8 us (10%)
  blocking collectives  39.8 us (8%)
  other arithmetic  15.5 us (3%)
  between operations  14 us (3%)
  local copies, waits for them, and re-layouts  8.87 us (2%)
    all_gather x2, waiting for transfers between devices, gather_hidden(): return lax.all_gather(stacked, 'row', axis=1, tiled=True)  112 us
    reduce_scatter x1, waiting for transfers between devices, per_device(): lax.psum_scatter(jnp.concatenate([jnp.dot(rows, gate_weight, preferred_el...  84.9 us
    reduce_scatter x1, waiting for transfers between devices, per_device(): lax.psum_scatter(right_transpose(rows, down_weight).astype(jnp.bfloat16),...  81.6 us
    reduce_scatter x2, waiting for transfers between devices, column_total(): lax.psum_scatter(term_fn(jnp.int32(0), count_rows * lax.axis_size('col'))...  34.6 us
    all_gather x2, blocking collectives, gather_tokens(): return lax.all_gather(block, 'col', axis=0, tiled=True)  23.5 us
    dot_general x3, matrix products, transpose_product(): lax.dot_general(left, right, (((0,), (0,)), ((), ())), preferred_element_...  18.3 us
    reduce_scatter x1, waiting for transfers between devices, per_device(): lax.psum_scatter(transpose_product(gathered, grads_all[1]).astype(jnp.bfl...  17.1 us
    all_gather x1, blocking collectives, per_device(): score = jnp.sum(lax.all_gather(partial_score, 'row'), axis=0)  16.3 us
  transfers between devices with their start and end apart: 9, of which 8 were waited for; matrix products, arithmetic and copies ran while one was open for 8% of the time, Pallas kernels for 0%

profile of v1, /device:TPU:1, one launch (start us, length us, event | category | flops | bytes accessed | tf_op | source)
XLA Modules:
  0.0 472.0 jit_solution(14559898675121205872)
XLA Ops:
  7.2 13.6 %all_gather.18 = bf16[512,512]{1,0:T(8,128)(2,1)S(1)} all-gather(bf16[128,512]{1,0:T(8,128)(2,1)} %param.8), channel_id=1, replica_groups=mesh['row'=16,'col'=4,'dp'=2] {'col'}, dimensions={0}, use_global_device_ids=true | all-gather | bytes 655360 | tf_op jit(solution)/shard_map/all_gather | solution.py:22
  20.8 4.3 convolution_convert_fusion.4
  25.1 3.9 convolution_convert_fusion.5
  29.0 6.0 %pad_maximum_fusion = bf16[512,7168]{1,0:T(8,128)(2,1)} fusion(bf16[512,3584]{1,0:T(8,128)(2,1)S(1)} %convolution_convert_fusion.4, bf16[512,3584]{1,0:T(8,128)(2,1)} %convolution_convert_fusion.5), kind=kLoop, calls=%fused_computation | loop fusion | flops 14680064 | bytes 14680064 | tf_op jit(solution)/shard_map/concatenate | solution.py:45
  35.1 84.9 %reduce-scatter.8.cloned.1.call-done = bf16[32,7168]{1,0:T(8,128)(2,1)} async-done(((bf16[512,7168]{1,0:T(8,128)(2,1)}), bf16[32,7168]{1,0:T(8,128)(2,1)}) %reduce-scatter.8.cloned.1.call-update) | async-done | bytes 458768 | tf_op jit(solution)/shard_map/reduce_scatter | solution.py:44
  122.0 50.6 %all-gather.8.cloned.1.call-done = bf16[512,3584]{1,0:T(8,128)(2,1)} async-done(((bf16[32,3584]{1,0:T(8,128)(2,1)}), bf16[512,3584]{1,0:T(8,128)(2,1)}) %all-gather.8.cloned.1.call-update) | async-done | bytes 3670032 | tf_op jit(solution)/shard_map/all_gather | solution.py:26
  172.7 6.0 %convolution_convert_fusion.6 = bf16[512,512]{1,0:T(8,128)(2,1)} fusion(bf16[512,3584]{1,0:T(8,128)(2,1)} %all-gather.8.cloned.1.call-done, bf16[3584,512]{1,0:T(8,128)(2,1)} %param.11), kind=kOutput, calls=%fused_computation.15 | convolution fusion | flops 1879310336 | bytes 7864320 | tf_op jit(solution)/shard_map/dot_general | solution.py:63
  178.8 19.6 %reduce-scatter.10.cloned.1.call-done = bf16[128,512]{1,0:T(8,128)(2,1)} async-done(((bf16[512,512]{1,0:T(8,128)(2,1)}), bf16[128,512]{1,0:T(8,128)(2,1)}) %reduce-scatter.10.cloned.1.call-update) | async-done | bytes 131088 | tf_op jit(solution)/shard_map/reduce_scatter | solution.py:30
  199.5 16.3 %all-gather.2 = f32[16,1,128]{2,1,0:T(1,128)S(1)} all-gather(f32[1,1,128]{2,1,0:T(1,128)S(1)} %convolution_bitcast_fusion), channel_id=3, replica_groups=mesh['row'=16,'col'=4,'dp'=2] {'row'}, dimensions={0}, use_global_device_ids=true | all-gather | bytes 8704 | tf_op jit(solution)/shard_map/all_gather | solution.py:69
  216.0 9.9 %all_gather.22 = bf16[512,512]{1,0:T(8,128)(2,1)S(1)} all-gather(bf16[128,512]{1,0:T(8,128)(2,1)S(1)} %fusion.14), channel_id=1, replica_groups=mesh['row'=16,'col'=4,'dp'=2] {'col'}, dimensions={0}, use_global_device_ids=true | all-gather | bytes 655360 | tf_op jit(solution)/shard_map/all_gather | solution.py:22
  225.9 6.0 %convolution_convert_fusion.3 = bf16[512,3584]{1,0:T(8,128)(2,1)} fusion(bf16[512,512]{1,0:T(8,128)(2,1)S(1)} %all_gather.22, bf16[3584,512]{1,0:T(8,128)(2,1)} %param.11), kind=kOutput, calls=%fused_computation.4 | convolution fusion | flops 1880883200 | bytes 7864320 | tf_op jit(solution)/shard_map/dot_general | solution.py:16
  232.0 81.6 %reduce-scatter.12.cloned.1.call-done = bf16[32,3584]{1,0:T(8,128)(2,1)} async-done(((bf16[512,3584]{1,0:T(8,128)(2,1)}), bf16[32,3584]{1,0:T(8,128)(2,1)}) %reduce-scatter.12.cloned.1.call-update) | async-done | bytes 229392 | tf_op jit(solution)/shard_map/reduce_scatter | solution.py:79
  315.6 6.0 %convolution_convert_fusion = bf16[3584,512]{1,0:T(8,128)(2,1)} fusion(bf16[512,3584]{1,0:T(8,128)(2,1)} %all-gather.8.cloned.1.call-done, bf16[512,512]{1,0:T(8,128)(2,1)S(1)} %all_gather.22), kind=kOutput, calls=%fused_computation.1 | convolution fusion | flops 1880883200 | bytes 7864320 | tf_op jit(solution)/shard_map/dot_general | solution.py:10
  321.6 61.8 %all-gather.6.cloned.1.call-done = bf16[2,512,3584]{2,1,0:T(8,128)(2,1)} async-done(((bf16[2,32,3584]{2,1,0:T(8,128)(2,1)}), bf16[2,512,3584]{2,1,0:T(8,128)(2,1)}) %all-gather.6.cloned.1.call-update) | async-done | bytes 7340048 | tf_op jit(solution)/shard_map/all_gather | solution.py:26
  383.4 5.4 %fusion.2 = f32[512,512]{1,0:T(8,128)S(1)} fusion(bf16[512,3584]{1,0:T(8,128)(2,1)} %param.9, bf16[2,512,3584]{2,1,0:T(8,128)(2,1)} %all-gather.6.cloned.1.call-done), kind=kOutput, calls=%fused_computation.11 | convolution fusion | flops 1879048192 | bytes 8388608 | tf_op jit(solution)/shard_map/dot_general | solution.py:16
  389.7 2.9 fusion.5
  392.8 6.0 %fusion.1 = bf16[512,3584]{0,1:T(8,128)(2,1)} fusion(bf16[512,512]{1,0:T(8,128)(2,1)S(1)} %all_gather.18, bf16[2,512,3584]{2,1,0:T(8,128)(2,1)} %all-gather.6.cloned.1.call-done), kind=kOutput, calls=%fused_computation.8 | convolution fusion | flops 1880883200 | bytes 7864320 | tf_op jit(solution)/shard_map/dot_general | solution.py:10
  398.9 6.3 %fusion = bf16[512,3584]{0,1:T(8,128)(2,1)} fusion(bf16[512,512]{1,0:T(8,128)(2,1)S(1)} %all_gather.18, bf16[2,512,3584]{2,1,0:T(8,128)(2,1)} %all-gather.6.cloned.1.call-done), kind=kOutput, calls=%fused_computation.7 | convolution fusion | flops 1880883200 | bytes 7864320 | tf_op jit(solution)/shard_map/dot_general | solution.py:10
  405.2 3.9 convert_element_type.94
  409.1 14.9 %reduce-scatter.20.cloned.1.call-done = bf16[128,512]{1,0:T(8,128)(2,1)} async-done(((bf16[512,512]{1,0:T(8,128)(2,1)}), bf16[128,512]{1,0:T(8,128)(2,1)}) %reduce-scatter.20.cloned.1.call-update) | async-done | bytes 131088 | tf_op jit(solution)/shard_map/reduce_scatter | solution.py:30
  425.7 17.1 %reduce-scatter.16.cloned.1.call-done = bf16[256,3584]{0,1:T(8,128)(2,1)} async-done(((bf16[512,3584]{0,1:T(8,128)(2,1)}), bf16[256,3584]{0,1:T(8,128)(2,1)}) %reduce-scatter.16.cloned.1.call-update) | async-done | bytes 1835024 | tf_op jit(solution)/shard_map/reduce_scatter | solution.py:102
  442.9 4.0 copy.15
  446.8 14.7 %reduce-scatter.14.cloned.1.call-done = bf16[256,3584]{0,1:T(8,128)(2,1)} async-done(((bf16[512,3584]{0,1:T(8,128)(2,1)}), bf16[256,3584]{0,1:T(8,128)(2,1)}) %reduce-scatter.14.cloned.1.call-update) | async-done | bytes 1835024 | tf_op jit(solution)/shard_map/reduce_scatter | solution.py:96
  461.5 4.0 copy.14
  (46 shorter events, 8.5 us)
Async XLA Ops:
  7.2 112.8 %reduce-scatter.8.cloned.1.call-start = ((), (), s32[]{:S(2)}) async-start(), calls=%async_computation.7 | async-start | bytes 7798784 | tf_op jit(solution)/shard_map/reduce_scatter | solution.py:44
  20.8 4.3 copy-start.6
  35.0 137.6 %all-gather.8.cloned.1.call-start = ((), (), s32[]{:S(2)}) async-start(), calls=%async_computation.15 | async-start | bytes 3899392 | tf_op jit(solution)/shard_map/all_gather | solution.py:26
  121.9 56.8 %copy-start.2 = (bf16[512]{0:T(512)(128)(2,1)S(1)}, bf16[512]{0:T(512)(128)(2,1)}, u32[]{:S(2)}) copy-start(bf16[512]{0:T(512)(128)(2,1)} %param.12) | copy-start | bytes 3076
  121.9 76.5 %copy-start = (bf16[128,512]{1,0:T(8,128)(2,1)S(1)}, bf16[128,512]{1,0:T(8,128)(2,1)}, u32[]{:S(2)}) copy-start(bf16[128,512]{1,0:T(8,128)(2,1)} %param.8) | copy-start | bytes 393220
  122.0 93.9 %copy-start.3 = (s32[128]{0:T(128)S(1)}, s32[128]{0:T(128)}, u32[]{:S(2)}) copy-start(s32[128]{0:T(128)} %param.14) | copy-start | bytes 1540
  122.0 93.9 %copy-start.4 = (s32[128]{0:T(128)S(1)}, s32[128]{0:T(128)}, u32[]{:S(2)}) copy-start(s32[128]{0:T(128)} %param.15) | copy-start | bytes 1540
  122.0 93.9 %copy-start.1 = (bf16[128,512]{1,0:T(8,128)(2,1)S(1)}, bf16[128,512]{1,0:T(8,128)(2,1)}, u32[]{:S(2)}) copy-start(bf16[128,512]{1,0:T(8,128)(2,1)} %param.13) | copy-start | bytes 393220
  122.0 76.4 %reduce-scatter.10.cloned.1.call-start = ((), (), s32[]{:S(2)}) async-start(), calls=%async_computation.8 | async-start | bytes 655360 | tf_op jit(solution)/shard_map/reduce_scatter | solution.py:30
  178.7 134.8 %reduce-scatter.12.cloned.1.call-start = ((), (), s32[]{:S(2)}) async-start(), calls=%async_computation.9 | async-start | bytes 3899392 | tf_op jit(solution)/shard_map/reduce_scatter | solution.py:79
  231.9 151.5 %all-gather.6.cloned.1.call-start = ((), (), s32[]{:S(2)}) async-start(), calls=%async_computation.10 | async-start | bytes 7798784 | tf_op jit(solution)/shard_map/all_gather | solution.py:26
  315.5 89.7 %reduce-scatter.18.cloned.1.call-start = ((), (), s32[]{:S(2)}) async-start(), calls=%async_computation.13 | async-start | bytes 5505024 | tf_op jit(solution)/shard_map/reduce_scatter | solution.py:108
  321.6 102.4 %reduce-scatter.20.cloned.1.call-start = ((), (), s32[]{:S(2)}) async-start(), calls=%async_computation.14 | async-start | bytes 655360 | tf_op jit(solution)/shard_map/reduce_scatter | solution.py:30
  383.4 5.4 %copy-start.5 = (bf16[2,512,3584]{2,1,0:T(8,128)(2,1)S(1)}, bf16[2,512,3584]{2,1,0:T(8,128)(2,1)}, u32[]{:S(2)}) copy-start(bf16[2,512,3584]{2,1,0:T(8,128)(2,1)} %all-gather.6.cloned.1.call-done) | copy-start | bytes 22020100
  383.4 6.3 %copy-start.7 = (bf16[512,3584]{1,0:T(8,128)(2,1)S(1)}, bf16[512,3584]{1,0:T(8,128)(2,1)}, u32[]{:S(2)}) copy-start(bf16[512,3584]{1,0:T(8,128)(2,1)} %param.10) | copy-start | bytes 11010052
  392.6 50.3 %reduce-scatter.16.cloned.1.call-start = ((), (), s32[]{:S(2)}) async-start(), calls=%async_computation.12 | async-start | bytes 5505024 | tf_op jit(solution)/shard_map/reduce_scatter | solution.py:102
  398.8 62.7 %reduce-scatter.14.cloned.1.call-start = ((), (), s32[]{:S(2)}) async-start(), calls=%async_computation.11 | async-start | bytes 5505024 | tf_op jit(solution)/shard_map/reduce_scatter | solution.py:96
Sparse Core Ops, SparseCore 0:
  35.1 84.8 reduce-scatter.7
  122.9 49.6 all-gather.7
  178.8 19.5 reduce-scatter.9
  232.0 81.4 reduce-scatter.11
  316.3 67.0 all-gather.5
  386.3 14.3 reduce-scatter.17
  403.1 20.8 reduce-scatter.19
  426.9 15.8 reduce-scatter.15
  445.9 15.5 reduce-scatter.13
